TPU v7x, 256 devices: a whole 4x4x8 slice. The times are simulated.
256 devices in a mesh: chan: 16 (over x, y), tm: 16 (over z, core).
Axes of the slice: x: 4, y: 4, z: 8, core: 2. Of those that a mesh axis runs over, the one named last changes fastest.
Arguments:
- records: bfloat16 [16, 6144, 1536], P('tm', 'chan')
- partners: int32 [16, 3], P('chan'), may hold values from 0 to 15, as said below
- counts: int32 [16], P('chan'), may hold values from 1 to 3, as said below
- sources: int32 [16, 2], P('chan'), may hold values from 0 to 383, as said below
Outputs:
- xcorr: float32 [16, 384, 3, 2, 384], P('chan', 'tm')
Inputs may be any that keep to these rules, and one draw needn't show every extreme that they name: `partners`: each row holds 3 different blocks. `counts`: some block has all 3 slots live. `sources`: each row holds 2 different channels.
All inputs are finite; a program needn't handle non-finite values.
Results may differ from a plain program's by a relative error of at most 0.008.
Values may be sent and summed in bfloat16 or wider, within the bound.
A program may use at most 64 MiB of HBM per device.

v0:
```python
import math
import jax
import jax.numpy as jnp
from jax import lax
from jax.sharding import PartitionSpec as P

L = 1536
F = 320
HL = 192
SMOOTH = 32


def dft_table(length, bins):
    sample_index = jnp.arange(length, dtype=jnp.int32)[:, None]
    bin_index = jnp.arange(bins, dtype=jnp.int32)[None, :] + 1
    phase_index = sample_index * bin_index % length
    angle = phase_index.astype(jnp.float32) * (2.0 * math.pi / length)
    return jnp.concatenate([jnp.cos(angle), -jnp.sin(angle)], axis=1).astype(jnp.bfloat16)


def lag_table(length, bins, half):
    bin_index = jnp.arange(bins, dtype=jnp.int32)[:, None] + 1
    lag_index = jnp.arange(2 * half, dtype=jnp.int32)[None, :] - half
    phase_index = jnp.mod(bin_index * lag_index, length)
    angle = phase_index.astype(jnp.float32) * (2.0 * math.pi / length)
    return jnp.concatenate([jnp.cos(angle), -jnp.sin(angle)], axis=0)


def band_table(bins, half):
    input_bin = jnp.arange(bins, dtype=jnp.int32)[:, None]
    output_bin = jnp.arange(bins, dtype=jnp.int32)[None, :]
    centre = jnp.clip(output_bin, half, bins - 1 - half)
    return (jnp.abs(input_bin - centre) <= half).astype(jnp.float32)


def whiten(block_records):
    windows, channels, length = block_records.shape
    signal = block_records.astype(jnp.float32)
    signal = signal - jnp.mean(signal, axis=-1, keepdims=True)
    demeaned = signal.astype(jnp.bfloat16).reshape(windows * channels, length)
    spectrum = jnp.dot(demeaned, dft_table(L, F), preferred_element_type=jnp.float32)
    real_part = spectrum[:, :F]
    imag_part = spectrum[:, F:]
    amplitude = jnp.sqrt(real_part * real_part + imag_part * imag_part)
    smooth = jnp.dot(amplitude, band_table(F, SMOOTH), precision=lax.Precision.HIGHEST) / (
        2 * SMOOTH + 1
    )
    factor = 1.0 / (smooth + 1e-06)
    whitened = jnp.concatenate([real_part * factor, imag_part * factor], axis=1)
    return whitened.astype(jnp.bfloat16).reshape(windows, channels, 2 * F)


def cross_terms(source_spec, partner_white):
    src_real = source_spec[..., :F]
    src_imag = source_spec[..., F:]
    rec_real = partner_white[..., :F]
    rec_imag = partner_white[..., F:]
    cross_real = jnp.einsum(
        "wsf,pwcf->cpsf", src_real, rec_real, preferred_element_type=jnp.float32
    ) + jnp.einsum("wsf,pwcf->cpsf", src_imag, rec_imag, preferred_element_type=jnp.float32)
    cross_imag = jnp.einsum(
        "wsf,pwcf->cpsf", src_real, rec_imag, preferred_element_type=jnp.float32
    ) - jnp.einsum("wsf,pwcf->cpsf", src_imag, rec_real, preferred_element_type=jnp.float32)
    return jnp.concatenate([cross_real, cross_imag], axis=-1)


def local(records, partners, counts, sources):
    windows, channels, length = records.shape
    slots = partners.shape[1]
    white = whiten(records)
    partner_ids = partners[0]
    live = jnp.arange(slots, dtype=jnp.int32) < counts[0]
    piece = lax.all_gather(white, "chan", axis=1, tiled=True)
    blocks_here = piece.shape[1] // channels
    block_ids = jnp.arange(blocks_here, dtype=jnp.int32)
    matches = ((block_ids[None, :] == partner_ids[:, None]) & live[:, None]).astype(jnp.bfloat16)
    shaped = piece.reshape(windows, blocks_here, channels, piece.shape[2])
    partner_white = jnp.einsum(
        "pj,wjcf->pwcf", matches, shaped, preferred_element_type=jnp.float32
    ).astype(jnp.bfloat16)
    picker = (jnp.arange(channels, dtype=jnp.int32)[None, :] == sources[0][:, None]).astype(
        jnp.bfloat16
    )
    source_spec = jnp.einsum(
        "sc,wcf->wsf", picker, white, preferred_element_type=jnp.float32
    ).astype(jnp.bfloat16)
    sources_count = source_spec.shape[1]
    inverse = lag_table(L, F, HL)
    scale = 1.0 / math.sqrt(F * windows * lax.axis_size("tm"))
    share_rows = channels // lax.axis_size("tm")
    stacked = cross_terms(source_spec, partner_white)
    summed = lax.psum_scatter(stacked, "tm", scatter_dimension=0, tiled=True)
    lagged = jnp.dot(
        summed.reshape(share_rows * slots * sources_count, 2 * F),
        inverse,
        precision=lax.Precision.HIGHEST,
    )
    result = lagged.reshape(share_rows, slots, sources_count, 2 * HL) * scale
    return result[None]


def solution(mesh):
    return jax.shard_map(
        local,
        mesh=mesh,
        in_specs=(P("tm", "chan", None), P("chan", None), P("chan"), P("chan", None)),
        out_specs=P("chan", "tm", None, None, None),
        check_vma=False,
    )
```

profile of v0, /device:TPU:2, one launch (start us, length us, event | category | flops | bytes accessed | tf_op | source)
XLA Modules:
  0.0 186.4 jit_solution(6916343911090276861)
XLA Ops:
  6.5 0.0 copy-start
  6.5 0.0 all-gather.2.cloned.1.call-start
  6.5 10.0 %cosine_convert_fusion = (bf16[1536,320]{1,0:T(8,128)(2,1)S(1)}, bf16[1536,320]{1,0:T(8,128)(2,1)S(1)}) fusion(s32[320]{0:T(512)S(1)} %iota_add_fusion.1), kind=kLoop, calls=%fused_computation.14 | loop fusion | flops 5898240 | bytes 1967360 | tf_op jit(solution)/shard_map/convert.30
  16.6 0.0 copy-done
  16.6 0.2 convert_reduce_fusion
  16.8 1.2 fusion.8
  18.0 0.0 copy-start.2
  18.0 0.0 copy-start.1
  18.0 1.1 multiply_convert_fusion.1
  19.1 1.0 pad_maximum_fusion.1
  20.0 0.0 all-gather.2.cloned.1.call-update
  20.1 0.2 reduce-scatter.2.cloned.1.call-start
  21.0 0.0 copy-done.2
  21.0 0.3 fusion.20
  21.2 0.1 convert_bitcast_fusion.4
  21.3 75.4 %all-gather.2.cloned.1.call-done = bf16[1,6144,640]{2,1,0:T(8,128)(2,1)} async-done(((bf16[1,384,640]{2,1,0:T(8,128)(2,1)}), bf16[1,6144,640]{2,1,0:T(8,128)(2,1)}) %all-gather.2.cloned.1.call-update) | async-done | bytes 7864336 | tf_op jit(solution)/shard_map/all_gather | solution.py:73
  96.7 0.0 copy-done.1
  96.7 7.9 %convert_bitcast_fusion.2 = bf16[3,1,384,640]{3,0,2,1:T(4,128)(2,1)S(1)} fusion(bf16[16,384,640]{2,1,0:T(8,128)(2,1)} %bitcast.59, s32[3]{0:T(128)S(1)} %bitcast.62, pred[3]{0:T(512)(128)(4,1)S(1)} %iota_compare_fusion.1), kind=kOutput, calls=%fused_computation.23 | convolution fusion | flops 24330336 | bytes 9338895 | tf_op jit(solution)/shard_map/pj,wjcf->pwcf/dot_general | solution.py:78
  104.6 1.2 convert_bitcast_fusion.1
  105.8 0.1 copy.7
  105.9 0.1 copy.8
  106.0 0.9 add_bitcast_fusion
  106.9 3.6 %pad_maximum_fusion = f32[384,3,2,640]{3,0,2,1:T(8,128)} fusion(f32[384,3,2,320]{3,0,2,1:T(8,128)S(1)} %get-tuple-element.6, f32[384,3,2,320]{3,0,2,1:T(8,128)S(1)} %get-tuple-element.5), kind=kLoop, calls=%fused_computation.2 | loop fusion | flops 1474560 | bytes 11796480 | tf_op jit(solution)/shard_map/concatenate | solution.py:64
  110.5 0.0 reduce-scatter.2.cloned.1.call-update
  110.6 2.1 %fusion.36 = (f32[320,384]{1,0:T(8,128)S(1)}, f32[320,384]{1,0:T(8,128)S(1)}) fusion(s32[384]{0:T(512)S(1)} %iota_add_fusion, s32[320]{0:T(512)S(1)} %iota_add_fusion.1), kind=kLoop, calls=%fused_computation.57 | loop fusion | flops 1228800 | bytes 985856 | tf_op jit(solution)/shard_map/cos | solution.py:26
  112.6 64.2 %reduce-scatter.2.cloned.1.call-done = f32[24,3,2,640]{3,0,2,1:T(8,128)} async-done(((f32[384,3,2,640]{3,0,2,1:T(8,128)}), f32[24,3,2,640]{3,0,2,1:T(8,128)}) %reduce-scatter.2.cloned.1.call-update) | async-done | bytes 368656 | tf_op jit(solution)/shard_map/reduce_scatter | solution.py:92
  176.8 1.9 %fusion.19 = f32[1,24,3,2,384]{4,1,3,2,0:T(8,128)S(1)} fusion(f32[24,3,2,640]{3,0,2,1:T(8,128)} %reduce-scatter.2.cloned.1.call-done, f32[320,384]{1,0:T(8,128)S(1)} %get-tuple-element.12, f32[320,384]{1,0:T(8,128)S(1)} %get-tuple-element.11), kind=kOutput, calls=%fused_computation.32 | convolution fusion | flops 424974336 | bytes 1572864 | tf_op jit(solution)/shard_map/dot_general | solution.py:93
  178.7 0.8 copy.9
  (5 shorter events, 0.0 us)
Async XLA Ops:
  6.5 10.0 %copy-start = (bf16[1,384,1536]{2,1,0:T(8,128)(2,1)S(1)}, bf16[1,384,1536]{2,1,0:T(8,128)(2,1)}, u32[]{:S(2)}) copy-start(bf16[1,384,1536]{2,1,0:T(8,128)(2,1)} %param.4) | copy-start | bytes 3538948
  6.5 90.1 %all-gather.2.cloned.1.call-start = ((), (), s32[]{:S(2)}) async-start(), calls=%async_computation.1 | async-start | bytes 8355840 | tf_op jit(solution)/shard_map/all_gather | solution.py:73
  18.0 3.0 %copy-start.2 = (s32[1,2]{1,0:T(1,128)S(1)}, s32[1,2]{1,0:T(1,128)}, u32[]{:S(2)}) copy-start(s32[1,2]{1,0:T(1,128)} %param.7) | copy-start | bytes 28
  18.0 78.7 %copy-start.1 = (s32[1,3]{1,0:T(1,128)S(1)}, s32[1,3]{1,0:T(1,128)}, u32[]{:S(2)}) copy-start(s32[1,3]{1,0:T(1,128)} %param.5) | copy-start | bytes 40
  20.1 156.7 %reduce-scatter.2.cloned.1.call-start = ((), (), s32[]{:S(2)}) async-start(), calls=%async_computation.2 | async-start | bytes 6266880 | tf_op jit(solution)/shard_map/reduce_scatter | solution.py:92
Sparse Core Ops, SparseCore 0:
  20.2 76.4 all-gather.1
  110.7 66.0 reduce-scatter.1
where the time goes:
time: 187 us; the launch traced here: 186 us
  waiting for transfers between devices  140 us (75%)
  other arithmetic  19.1 us (10%)
  between operations  14.2 us (8%)
  matrix products  12.3 us (7%)
    all_gather x1, waiting for transfers between devices, local(): piece = lax.all_gather(white, 'chan', axis=1, tiled=True)  75.4 us
    reduce_scatter x1, waiting for transfers between devices, local(): summed = lax.psum_scatter(stacked, 'tm', scatter_dimension=0, tiled=True)  64.2 us
    another operation x3, other arithmetic  11.2 us
    dot_general x1, matrix products, local(): jnp.einsum('pj,wjcf->pwcf', matches, shaped, preferred_element_type=jnp.f...  7.9 us
  transfers between devices with their start and end apart: 2, of which 2 were waited for; matrix products, arithmetic and copies ran while one was open for 1% of the time, Pallas kernels for 0%

commit v1 on v0

--- a/solution.py
+++ b/solution.py
@@ -70,7 +70,9 @@
     white = whiten(records)
     partner_ids = partners[0]
     live = jnp.arange(slots, dtype=jnp.int32) < counts[0]
-    piece = lax.all_gather(white, "chan", axis=1, tiled=True)
+    piece = jnp.concatenate(
+        lax.all_to_all(jnp.stack([white] * lax.axis_size("chan")), "chan", 0, 0), axis=1
+    )
     blocks_here = piece.shape[1] // channels
     block_ids = jnp.arange(blocks_here, dtype=jnp.int32)
     matches = ((block_ids[None, :] == partner_ids[:, None]) & live[:, None]).astype(jnp.bfloat16)

time: 187 us -> 263 us (1.41)
  waiting for transfers between devices: 140 us -> 205 us
  starting transfers between devices: 0.22 us -> 7.83 us
  local copies, waits for them, and re-layouts: 1.05 us -> 5.11 us
    all_to_all x0 -> x1, waiting for transfers between devices: none -> 97.3 us  [local(): lax.all_to_all(jnp.stack([white] * lax.axis_size('chan')), 'chan', 0, 0)]
    all_gather x1 -> x0, waiting for transfers between devices: 75.4 us -> none  [local(): piece = lax.all_gather(white, 'chan', axis=1, tiled=True)]
    reduce_scatter x1, waiting for transfers between devices: 64.2 us -> 108 us  [local(): summed = lax.psum_scatter(stacked, 'tm', scatter_dimension=0, tiled=True)]
    all_to_all x0 -> x1, starting transfers between devices: none -> 7.61 us  [local(): lax.all_to_all(jnp.stack([white] * lax.axis_size('chan')), 'chan', 0, 0)]
    another operation x2 -> x3, local copies, waits for them, and re-layouts: 0.23 us -> 4.3 us  [the longest x1 4.07 us: local(): jnp.stack([white] * lax.axis_size('chan'))]
where the time goes in v1:
time: 263 us
  waiting for transfers between devices  205 us (78%)
  other arithmetic  18.2 us (7%)
  between operations  14.1 us (5%)
  matrix products  12.2 us (5%)
  starting transfers between devices  7.83 us (3%)
  local copies, waits for them, and re-layouts  5.11 us (2%)
    reduce_scatter x1, waiting for transfers between devices, local(): summed = lax.psum_scatter(stacked, 'tm', scatter_dimension=0, tiled=True)  108 us
    all_to_all x1, waiting for transfers between devices, local(): lax.all_to_all(jnp.stack([white] * lax.axis_size('chan')), 'chan', 0, 0)  97.3 us
    another operation x3, other arithmetic  11.2 us
    dot_general x1, matrix products, local(): jnp.einsum('pj,wjcf->pwcf', matches, shaped, preferred_element_type=jnp.f...  7.9 us
    all_to_all x1, starting transfers between devices, local(): lax.all_to_all(jnp.stack([white] * lax.axis_size('chan')), 'chan', 0, 0)  7.61 us
  transfers between devices with their start and end apart: 2, of which 2 were waited for; matrix products, arithmetic and copies ran while one was open for 1% of the time, Pallas kernels for 0%

profile of v1, /device:TPU:2, one launch (start us, length us, event | category | flops | bytes accessed | tf_op | source)
XLA Modules:
  0.0 262.8 jit_solution(18332548738708405152)
XLA Ops:
  6.5 0.0 copy-start
  6.5 10.0 %cosine_convert_fusion = (bf16[1536,320]{1,0:T(8,128)(2,1)S(1)}, bf16[1536,320]{1,0:T(8,128)(2,1)S(1)}) fusion(s32[320]{0:T(512)S(1)} %iota_add_fusion.1), kind=kLoop, calls=%fused_computation.15 | loop fusion | flops 5898240 | bytes 1967360 | tf_op jit(solution)/shard_map/convert.26
  16.5 0.0 copy-done
  16.6 0.2 convert_reduce_fusion
  16.8 1.2 fusion.9
  18.0 1.1 multiply_convert_fusion.1
  19.0 0.2 pad_maximum_fusion.1
  19.2 4.1 %stack.3 = bf16[16,1,384,640]{3,2,1,0:T(8,128)(2,1)} broadcast(bf16[384,640]{1,0:T(8,128)(2,1)S(1)} %pad_maximum_fusion.1), dimensions={2,3} | broadcast | bytes 8355840 | tf_op jit(solution)/shard_map/stack | solution.py:74
  23.3 0.0 copy-start.2
  23.3 0.0 copy-start.1
  23.3 7.6 %all-to-all-start = ((bf16[16,1,384,640]{3,2,1,0:T(8,128)(2,1)}), bf16[16,1,384,640]{3,2,1,0:T(8,128)(2,1)}, u32[]{:S(2)}, u32[]{:S(2)}) async-start(bf16[16,1,384,640]{3,2,1,0:T(8,128)(2,1)} %stack.3), calls=%async_computation | async-start | bytes 15728640 | tf_op jit(solution)/shard_map/all_to_all | solution.py:74
  30.9 0.2 reduce-scatter.2.cloned.1.call-start
  31.8 0.0 copy-done.2
  31.8 0.2 fusion.21
  32.0 0.1 convert_bitcast_fusion.4
  32.1 97.3 %all-to-all-done = bf16[16,1,384,640]{3,2,1,0:T(8,128)(2,1)} async-done(((bf16[16,1,384,640]{3,2,1,0:T(8,128)(2,1)}), bf16[16,1,384,640]{3,2,1,0:T(8,128)(2,1)}, u32[]{:S(2)}, u32[]{:S(2)}) %all-to-all-start) | async-done | bytes 7864352 | tf_op jit(solution)/shard_map/all_to_all | solution.py:74
  129.4 0.0 copy-done.1
  129.4 7.9 %convert_bitcast_fusion.2 = bf16[3,1,384,640]{3,0,2,1:T(4,128)(2,1)S(1)} fusion(bf16[16,1,384,640]{3,2,1,0:T(8,128)(2,1)} %all-to-all-done, s32[3]{0:T(128)S(1)} %bitcast.62, pred[3]{0:T(512)(128)(4,1)S(1)} %iota_compare_fusion.1), kind=kOutput, calls=%fused_computation.24 | convolution fusion | flops 24330336 | bytes 9338895 | tf_op jit(solution)/shard_map/pj,wjcf->pwcf/dot_general | solution.py:80
  137.3 1.2 convert_bitcast_fusion.1
  138.4 0.1 copy.12
  138.6 0.1 copy.11
  138.7 0.9 add_bitcast_fusion
  139.6 3.6 %pad_maximum_fusion = f32[384,3,2,640]{3,0,2,1:T(8,128)} fusion(f32[384,3,2,320]{3,0,2,1:T(8,128)S(1)} %get-tuple-element.6, f32[384,3,2,320]{3,0,2,1:T(8,128)S(1)} %get-tuple-element.5), kind=kLoop, calls=%fused_computation.3 | loop fusion | flops 1474560 | bytes 11796480 | tf_op jit(solution)/shard_map/concatenate | solution.py:64
  143.2 0.0 reduce-scatter.2.cloned.1.call-update
  143.2 2.1 fusion.34
  145.3 107.9 %reduce-scatter.2.cloned.1.call-done = f32[24,3,2,640]{3,0,2,1:T(8,128)} async-done(((f32[384,3,2,640]{3,0,2,1:T(8,128)}), f32[24,3,2,640]{3,0,2,1:T(8,128)}) %reduce-scatter.2.cloned.1.call-update) | async-done | bytes 368656 | tf_op jit(solution)/shard_map/reduce_scatter | solution.py:94
  253.2 1.9 fusion.20
  255.1 0.8 copy.13
  (5 shorter events, 0.0 us)
Async XLA Ops:
  6.5 10.0 %copy-start = (bf16[1,384,1536]{2,1,0:T(8,128)(2,1)S(1)}, bf16[1,384,1536]{2,1,0:T(8,128)(2,1)}, u32[]{:S(2)}) copy-start(bf16[1,384,1536]{2,1,0:T(8,128)(2,1)} %param.4) | copy-start | bytes 3538948
  23.3 8.5 %copy-start.2 = (s32[1,2]{1,0:T(1,128)S(1)}, s32[1,2]{1,0:T(1,128)}, u32[]{:S(2)}) copy-start(s32[1,2]{1,0:T(1,128)} %param.7) | copy-start | bytes 28
  23.3 106.1 %copy-start.1 = (s32[1,3]{1,0:T(1,128)S(1)}, s32[1,3]{1,0:T(1,128)}, u32[]{:S(2)}) copy-start(s32[1,3]{1,0:T(1,128)} %param.5) | copy-start | bytes 40
  23.3 106.1 %all-to-all-start = ((bf16[16,1,384,640]{3,2,1,0:T(8,128)(2,1)}), bf16[16,1,384,640]{3,2,1,0:T(8,128)(2,1)}, u32[]{:S(2)}, u32[]{:S(2)}) async-start(bf16[16,1,384,640]{3,2,1,0:T(8,128)(2,1)} %stack.3), calls=%async_computation | async-start | bytes 15728640 | tf_op jit(solution)/shard_map/all_to_all | solution.py:74
  30.9 222.4 %reduce-scatter.2.cloned.1.call-start = ((), (), s32[]{:S(2)}) async-start(), calls=%async_computation.2 | async-start | bytes 6266880 | tf_op jit(solution)/shard_map/reduce_scatter | solution.py:94
Sparse Core Ops, SparseCore 0:
  143.3 109.8 reduce-scatter.1
